TPU v7x, 512 devices: a whole 4x4x16 slice. The times are simulated.
512 devices in a mesh: dp: 16 (over x, y), tm: 32 (over z, core).
Axes of the slice: x: 4, y: 4, z: 16, core: 2. Of those that a mesh axis runs over, the one named last changes fastest.
Arguments:
- records: bfloat16 [16, 4096, 1024], P('dp', 'tm'), may hold values from -6 to 6
- x_weight: bfloat16 [1024, 512], replicated, may hold values from -0.1875 to 0.1875
- bc_weight: bfloat16 [1024, 256], replicated, may hold values from -0.1875 to 0.1875
- decay_codes: int32 [16, 4096, 8], P('dp', 'tm'), may hold values from 0 to 524
- out_grad: bfloat16 [16, 4096, 512], P('dp', 'tm'), may hold values from -6 to 6
Outputs:
- y_out: bfloat16 [16, 4096, 512], P('dp', 'tm')
- x_grad: float32 [1024, 512], P('tm')
- bc_grad: float32 [1024, 256], P('tm')
All inputs are finite; a program needn't handle non-finite values.
Results may differ from a plain program's by a relative error of at most 0.0085.
Values sent between devices are 32-bit elements; how exact they have to be, the bound alone decides.
No kernel may reach another device: no remote copies, remote signals or barrier semaphores. Data moves between devices by JAX's collectives and lax.ppermute only.
A program may use at most 64 MiB of HBM per device.

v0:
```python
import jax
import jax.numpy as jnp
from jax import lax
from jax.sharding import PartitionSpec as P

SPAN = 128
highest = lax.Precision.HIGHEST


def entering(part, axis, combine, identity, reverse):
    count = lax.axis_size(axis)
    place = lax.axis_index(axis)
    ahead = count - 1 - place if reverse else place
    gathered = jax.tree.map(lambda a: lax.all_gather(a, axis), part)
    state = jax.tree.map(lambda a, e: jnp.zeros_like(a) + jnp.asarray(e, a.dtype), part, identity)

    def one(turn, state):
        source = count - 1 - turn if reverse else turn
        return combine(
            state, jax.tree.map(lambda a: lax.dynamic_index_in_dim(a, source, 0, False), gathered)
        )

    return lax.fori_loop(0, ahead, one, state)


def span_kernel(log_decay):
    running = jnp.cumsum(log_decay, axis=1)
    length = log_decay.shape[1]
    causal = lax.broadcasted_iota(jnp.int32, (length, length), 0) >= lax.broadcasted_iota(
        jnp.int32, (length, length), 1
    )
    causal = causal[None, None, :, :]
    heads_first = jnp.transpose(running, (0, 2, 1))
    gaps = heads_first[:, :, :, None] - heads_first[:, :, None, :]
    kernel = jnp.where(causal, jnp.exp(jnp.where(causal, gaps, 0.0)), 0.0)
    return (running, kernel)


def block_scores(readout, inject):
    return jnp.einsum(
        "rtn,rsn->rts",
        readout.astype(jnp.bfloat16),
        inject.astype(jnp.bfloat16),
        preferred_element_type=jnp.float32,
    )


def forward_span(carry_state, pieces):
    mixer_f, inject, readout, cot_heads, log_decay = pieces
    running, kernel = span_kernel(log_decay)
    scores = block_scores(readout, inject)
    mixing = kernel * scores[:, None, :, :]
    decayed = jnp.exp(running)
    within = jnp.einsum("rhts,rshp->rthp", mixing, mixer_f, precision=highest)
    carried = decayed[..., None] * jnp.einsum(
        "rhpn,rtn->rthp", carry_state, readout, precision=highest
    )
    pair_dots = jnp.einsum("rthp,rshp->rhts", cot_heads, mixer_f, precision=highest)
    grad_read = jnp.einsum("rhts,rsn->rtn", kernel * pair_dots, inject, precision=highest)
    grad_read = grad_read + jnp.einsum(
        "rthp,rhpn->rtn", decayed[..., None] * cot_heads, carry_state, precision=highest
    )
    to_end = jnp.exp(running[:, -1:, :] - running)
    new_state = jnp.exp(running[:, -1, :])[:, :, None, None] * carry_state
    new_state = new_state + jnp.einsum(
        "rshp,rsn->rhpn", to_end[..., None] * mixer_f, inject, precision=highest
    )
    return (new_state, (within + carried, grad_read))


def reverse_span(adjoint, pieces):
    mixer_f, inject, readout, cot_heads, log_decay = pieces
    running, kernel = span_kernel(log_decay)
    scores = block_scores(readout, inject)
    mixing = kernel * scores[:, None, :, :]
    pair_dots = jnp.einsum("rthp,rshp->rhts", cot_heads, mixer_f, precision=highest)
    to_end = jnp.exp(running[:, -1:, :] - running)
    grad_mixer = jnp.einsum("rhts,rthp->rshp", mixing, cot_heads, precision=highest)
    grad_mixer = grad_mixer + to_end[..., None] * jnp.einsum(
        "rhpn,rsn->rshp", adjoint, inject, precision=highest
    )
    grad_inject = jnp.einsum("rhts,rtn->rsn", kernel * pair_dots, readout, precision=highest)
    grad_inject = grad_inject + jnp.einsum(
        "rshp,rhpn->rsn", to_end[..., None] * mixer_f, adjoint, precision=highest
    )
    new_adjoint = jnp.exp(running[:, -1, :])[:, :, None, None] * adjoint
    new_adjoint = new_adjoint + jnp.einsum(
        "rthp,rtn->rhpn", jnp.exp(running)[..., None] * cot_heads, readout, precision=highest
    )
    return (new_adjoint, (grad_mixer, grad_inject))


def to_blocks(array, frames):
    return array.reshape((frames // SPAN, 1, SPAN) + array.shape[1:])


def combine_pair(earlier, later_one):
    return (earlier[0] * later_one[0], later_one[0][:, :, None, None] * earlier[1] + later_one[1])


def body(records, x_weight, bc_weight, decay_codes, out_grad):
    signal = records[0]
    codes = decay_codes[0]
    frames_dev, model_dim = signal.shape
    head_count = codes.shape[1]
    mixer_dim = x_weight.shape[1]
    head_size = mixer_dim // head_count
    state_size = bc_weight.shape[1] // 2
    tm_count = lax.axis_size("tm")
    groups = lax.axis_size("dp")
    out_scale = (state_size * frames_dev * tm_count) ** (-0.5)
    grad_scale = (groups * frames_dev * tm_count) ** (-0.5)
    decay_unit = 1.0 / (32.0 * frames_dev * tm_count)
    mixer_in = jnp.dot(signal, x_weight, preferred_element_type=jnp.float32).astype(jnp.bfloat16)
    state_proj = jnp.dot(signal, bc_weight, preferred_element_type=jnp.float32).astype(jnp.bfloat16)
    log_decay = -decay_unit * codes.astype(jnp.float32)
    cotangent = out_grad[0].astype(jnp.float32) * out_scale
    mixer_f = mixer_in.astype(jnp.float32).reshape(frames_dev, head_count, head_size)
    inject = state_proj[:, :state_size].astype(jnp.float32)
    readout = state_proj[:, state_size:].astype(jnp.float32)
    cot_heads = cotangent.reshape(frames_dev, head_count, head_size)
    blocks = (
        to_blocks(mixer_f, frames_dev),
        to_blocks(inject, frames_dev),
        to_blocks(readout, frames_dev),
        to_blocks(cot_heads, frames_dev),
        to_blocks(log_decay, frames_dev),
    )
    zero_state = jnp.zeros((1, head_count, head_size, state_size), jnp.float32)
    end_state, (local_out, local_read) = lax.scan(forward_span, zero_state, blocks)
    start_adjoint, (local_grad, local_inject) = lax.scan(
        reverse_span, zero_state, blocks, reverse=True
    )
    running = jnp.cumsum(log_decay, axis=0)
    device_log = running[-1]
    identity = (jnp.ones((1, head_count), jnp.float32), zero_state)
    carry_in = entering(
        (jnp.exp(device_log)[None], end_state), "tm", combine_pair, identity, False
    )[1][0]
    adjoint_in = entering(
        (jnp.exp(device_log)[None], start_adjoint), "tm", combine_pair, identity, True
    )[1][0]
    decayed = jnp.exp(running)
    to_end = jnp.exp(device_log[None] - running)
    output = local_out.reshape(frames_dev, head_count, head_size)
    output = output + decayed[..., None] * jnp.einsum(
        "hpn,tn->thp", carry_in, readout, precision=highest
    )
    grad_read = local_read.reshape(frames_dev, state_size)
    grad_read = grad_read + jnp.einsum(
        "thp,hpn->tn", decayed[..., None] * cot_heads, carry_in, precision=highest
    )
    grad_mixer = local_grad.reshape(frames_dev, head_count, head_size)
    grad_mixer = grad_mixer + to_end[..., None] * jnp.einsum(
        "hpn,tn->thp", adjoint_in, inject, precision=highest
    )
    grad_inject = local_inject.reshape(frames_dev, state_size)
    grad_inject = grad_inject + jnp.einsum(
        "thp,hpn->tn", to_end[..., None] * mixer_f, adjoint_in, precision=highest
    )
    grad_mix = grad_mixer.reshape(frames_dev, mixer_dim).astype(jnp.bfloat16)
    grad_proj = jnp.concatenate([grad_inject, grad_read], axis=1).astype(jnp.bfloat16)
    grad_cat = jnp.concatenate([grad_mix, grad_proj], axis=1)
    grad_share = lax.psum_scatter(
        lax.dot_general(
            signal, grad_cat, (((0,), (0,)), ((), ())), preferred_element_type=jnp.float32
        ),
        "tm",
        scatter_dimension=0,
        tiled=True,
    )
    grad_share = lax.psum(grad_share, "dp")
    grad_share = grad_share * grad_scale
    y_out = output.reshape(frames_dev, mixer_dim).astype(jnp.bfloat16)[None]
    return (y_out, grad_share[:, :mixer_dim], grad_share[:, mixer_dim:])


def solution(mesh):
    return jax.shard_map(
        body,
        mesh=mesh,
        in_specs=(P("dp", "tm", None), P(), P(), P("dp", "tm", None), P("dp", "tm", None)),
        out_specs=(P("dp", "tm", None), P("tm", None), P("tm", None)),
        check_vma=False,
    )
```

profile of v0, /device:TPU:32, one launch (start us, length us, event | category | flops | bytes accessed | tf_op | source)
XLA Modules:
  0.0 444.9 jit_solution(17753559127679987640)
XLA Ops:
  7.2 0.8 fusion.69
  9.1 1.4 convolution_convert_fusion.1
  10.5 1.3 convert_multiply_fusion
  11.9 1.0 convolution_add_fusion.1
  13.0 1.0 copy.79
  14.1 1.0 convolution_add_fusion
  15.5 33.9 %all-gather.3 = f32[32,1,8]{2,1,0:T(1,128)S(1)} all-gather(f32[1,1,8]{2,1,0:T(1,128)S(1)} %get-tuple-element.267), channel_id=2, replica_groups=mesh['dp'=16,'tm'=32] {'tm'}, dimensions={0}, use_global_device_ids=true | all-gather | bytes 1056 | tf_op jit(solution)/shard_map/all_gather | solution.py:14
  49.5 0.3 fusion.2
  49.8 0.4 convolution_bitcast_fusion.4
  50.2 0.4 convolution_bitcast_fusion.6
  50.6 0.7 fusion
  51.4 0.8 fusion.4
  52.1 44.4 %all-gather.7.cloned.1.call-done = f32[256,64,128]{2,1,0:T(8,128)} async-done(((f32[8,64,128]{2,1,0:T(8,128)}), f32[256,64,128]{2,1,0:T(8,128)}) %all-gather.7.cloned.1.call-update) | async-done | bytes 8388624 | tf_op jit(solution)/shard_map/all_gather | solution.py:14
  96.6 2.2 while.16
  96.6 1.1 bitcast_add_fusion.4
  97.7 1.1 bitcast_add_fusion.4
  98.8 76.1 %all-gather.9.cloned.1.call-done = f32[256,64,128]{2,1,0:T(8,128)} async-done(((f32[8,64,128]{2,1,0:T(8,128)}), f32[256,64,128]{2,1,0:T(8,128)}) %all-gather.9.cloned.1.call-update) | async-done | bytes 8388624 | tf_op jit(solution)/shard_map/all_gather | solution.py:14
  174.9 31.9 %while.17 = (s32[]{:T(128)}, f32[1,8,64,128]{3,2,1,0:T(8,128)S(1)}, s32[]{:T(128)}, f32[32,1,8]{2,1,0:T(1,128)S(1)}, f32[32,1,8,64,128]{4,3,2,1,0:T(8,128)}, /*index=5*/s32[]{:T(128)}, s32[]{:T(128)}, s32[]{:T(128)}, s32[]{:T(128)}) while((s32[]{:T(128)}, f32[1,8,64,128]{3,2,1,0:T(8,128)S(1)}, s32[]{:T(128)}, f32[32,1,8]{2,1,0:T(1,128)S(1)}, ...), condition=%wide.region_5.6_spmd, body=%wide.region_4.5_spmd.sunk | while | flops 131078 | bytes 786683 | solution.py:23
  174.9 1.1 bitcast_add_fusion.5
  176.0 1.1 bitcast_add_fusion.5
  177.1 1.1 bitcast_add_fusion.5
  178.2 1.1 bitcast_add_fusion.5
  179.3 1.1 bitcast_add_fusion.5
  180.4 1.1 bitcast_add_fusion.5
  181.5 1.1 bitcast_add_fusion.5
  182.6 1.1 bitcast_add_fusion.5
  183.7 1.1 bitcast_add_fusion.5
  184.8 1.1 bitcast_add_fusion.5
  185.9 1.1 bitcast_add_fusion.5
  187.0 1.1 bitcast_add_fusion.5
  188.1 1.1 bitcast_add_fusion.5
  189.2 1.1 bitcast_add_fusion.5
  190.4 1.1 bitcast_add_fusion.5
  191.5 1.1 bitcast_add_fusion.5
  192.6 1.1 bitcast_add_fusion.5
  193.7 1.1 bitcast_add_fusion.5
  194.8 1.1 bitcast_add_fusion.5
  195.9 1.1 bitcast_add_fusion.5
  197.0 1.1 bitcast_add_fusion.5
  198.1 1.1 bitcast_add_fusion.5
  199.2 1.1 bitcast_add_fusion.5
  200.3 1.1 bitcast_add_fusion.5
  201.4 1.1 bitcast_add_fusion.5
  202.5 1.1 bitcast_add_fusion.5
  203.6 1.1 bitcast_add_fusion.5
  204.7 1.1 bitcast_add_fusion.5
  205.8 1.1 bitcast_add_fusion.5
  206.8 0.6 convolution_bitcast_fusion.5
  207.4 0.3 fusion.10
  207.7 0.6 convolution_bitcast_fusion.3
  208.3 0.2 fusion.14
  208.6 0.2 fusion.13
  208.8 2.2 convolution_bitcast_fusion
  211.1 3.5 copy.87
  214.7 0.3 fusion.6
  214.9 0.7 fusion.8
  215.7 101.2 %reduce-scatter.4.cloned.1.call-done = f32[32,768]{1,0:T(8,128)} async-done(((f32[1024,768]{1,0:T(8,128)}), f32[32,768]{1,0:T(8,128)}) %reduce-scatter.4.cloned.1.call-update) | async-done | bytes 98320
  316.9 1.8 copy.88
  318.7 0.3 fusion.9
  319.0 0.8 copy.84
  319.7 116.2 %all-reduce.2.cloned.1.call-done = f32[32,768]{0,1:T(8,128)} async-done(((f32[32,768]{0,1:T(8,128)}), f32[32,768]{0,1:T(8,128)}) %all-reduce.2.cloned.1.call-update) | async-done | bytes 98320 | tf_op jit(solution)/shard_map/psum | solution.py:172
  435.9 1.0 broadcast_multiply_fusion
  437.0 0.7 copy.85
  437.7 0.7 copy.86
  (70 shorter events, 2.3 us)
Async XLA Ops:
  7.2 3.3 copy-start
  7.2 89.4 %all-gather.7.cloned.1.call-start = ((), (), s32[]{:S(2)}) async-start(), calls=%async_computation.2 | async-start | bytes 8650752 | tf_op jit(solution)/shard_map/all_gather | solution.py:14
  12.9 161.9 %all-gather.9.cloned.1.call-start = ((), (), s32[]{:S(2)}) async-start(), calls=%async_computation.3 | async-start | bytes 8650752 | tf_op jit(solution)/shard_map/all_gather | solution.py:14
  14.1 194.7 %copy-start.1 = (bf16[1,128,1024]{2,1,0:T(8,128)(2,1)S(1)}, bf16[1,128,1024]{2,1,0:T(8,128)(2,1)}, u32[]{:S(2)}) copy-start(bf16[1,128,1024]{2,1,0:T(8,128)(2,1)} %param.9) | copy-start | bytes 786436
  15.1 301.7 %reduce-scatter.4.cloned.1.call-start = ((), (), s32[]{:S(2)}) async-start(), calls=%async_computation.4 | async-start | bytes 3244032
  214.6 221.3 %all-reduce.2.cloned.1.call-start = ((), (), s32[]{:S(2)}) async-start(), calls=%async_computation.1 | async-start | bytes 786432 | tf_op jit(solution)/shard_map/psum | solution.py:172
Sparse Core Ops, SparseCore 0:
  13.0 83.4 all-gather.6
  98.7 76.1 all-gather.8
  214.7 102.0 reduce-scatter.3
  320.3 115.5 all-reduce.1
where the time goes:
time: 446 us; the launch traced here: 445 us
  waiting for transfers between devices  338 us (76%)
  other arithmetic  35.2 us (8%)
  blocking collectives  33.9 us (8%)
  between operations  14 us (3%)
  matrix products  12.6 us (3%)
  local copies, waits for them, and re-layouts  10 us (2%)
    all_gather x2, waiting for transfers between devices, entering(): gathered = jax.tree.map(lambda a: lax.all_gather(a, axis), part)  121 us
    psum x1, waiting for transfers between devices, body(): grad_share = lax.psum(grad_share, 'dp')  116 us
    unnamed x5, waiting for transfers between devices  101 us
    all_gather x1, blocking collectives, entering(): gathered = jax.tree.map(lambda a: lax.all_gather(a, axis), part)  33.9 us
    add x31, other arithmetic, combine_pair(): later_one[0][:, :, None, None] * earlier[1] + later_one[1]  32.9 us
  transfers between devices with their start and end apart: 4, of which 4 were waited for; matrix products, arithmetic and copies ran while one was open for 2% of the time, Pallas kernels for 0%

commit v1 on v0

--- a/solution.py
+++ b/solution.py
@@ -169,7 +169,7 @@
         scatter_dimension=0,
         tiled=True,
     )
-    grad_share = lax.psum(grad_share, "dp")
+    grad_share = jnp.sum(lax.all_gather(grad_share, "dp"), axis=0)
     grad_share = grad_share * grad_scale
     y_out = output.reshape(frames_dev, mixer_dim).astype(jnp.bfloat16)[None]
     return (y_out, grad_share[:, :mixer_dim], grad_share[:, mixer_dim:])

time: 446 us -> 391 us (0.88)
  the two profiles are of different devices: /device:TPU:32 before, /device:TPU:1 now
where the time goes in v1:
time: 391 us; the launch traced here: 390 us
  waiting for transfers between devices  281 us (72%)
  blocking collectives  37.4 us (10%)
  other arithmetic  35.7 us (9%)
  between operations  14 us (4%)
  matrix products  12.6 us (3%)
  local copies, waits for them, and re-layouts  7.99 us (2%)
    all_gather x2, waiting for transfers between devices, entering(): gathered = jax.tree.map(lambda a: lax.all_gather(a, axis), part)  120 us
    reduce_scatter x1, waiting for transfers between devices, body(): lax.psum_scatter(lax.dot_general(signal, grad_cat, (((0,), (0,)), ((), ()...  101 us
    all_gather x1, waiting for transfers between devices, body(): grad_share = jnp.sum(lax.all_gather(grad_share, 'dp'), axis=0)  59.9 us
    all_gather x1, blocking collectives, entering(): gathered = jax.tree.map(lambda a: lax.all_gather(a, axis), part)  37.4 us
    add x31, other arithmetic, combine_pair(): later_one[0][:, :, None, None] * earlier[1] + later_one[1]  32.9 us
  transfers between devices with their start and end apart: 4, of which 4 were waited for; matrix products, arithmetic and copies ran while one was open for 2% of the time, Pallas kernels for 0%

profile of v1, /device:TPU:1, one launch (start us, length us, event | category | flops | bytes accessed | tf_op | source)
XLA Modules:
  0.0 389.6 jit_solution(6191505337869478765)
XLA Ops:
  7.2 0.8 fusion.69
  8.1 0.2 reduce_window_sum.27
  9.1 1.4 convolution_convert_fusion.1
  10.5 1.3 convert_multiply_fusion
  11.9 1.0 convolution_add_fusion.1
  13.0 1.0 copy.75
  14.1 1.0 convolution_add_fusion
  15.5 37.4 %all-gather.4 = f32[32,1,8]{2,1,0:T(1,128)S(1)} all-gather(f32[1,1,8]{2,1,0:T(1,128)S(1)} %get-tuple-element.267), channel_id=2, replica_groups=mesh['dp'=16,'tm'=32] {'tm'}, dimensions={0}, use_global_device_ids=true | all-gather | bytes 1056 | tf_op jit(solution)/shard_map/all_gather | solution.py:14
  52.9 0.3 fusion.2
  53.2 0.4 convolution_bitcast_fusion.4
  53.6 0.4 convolution_bitcast_fusion.6
  54.0 0.7 fusion
  54.8 0.8 fusion.4
  55.5 42.9 %all-gather.9.cloned.1.call-done = f32[256,64,128]{2,1,0:T(8,128)} async-done(((f32[8,64,128]{2,1,0:T(8,128)}), f32[256,64,128]{2,1,0:T(8,128)}) %all-gather.9.cloned.1.call-update) | async-done | bytes 8388624 | tf_op jit(solution)/shard_map/all_gather | solution.py:14
  98.4 1.1 while.16
  98.5 1.1 bitcast_add_fusion.4
  99.5 77.1 %all-gather.11.cloned.1.call-done = f32[256,64,128]{2,1,0:T(8,128)} async-done(((f32[8,64,128]{2,1,0:T(8,128)}), f32[256,64,128]{2,1,0:T(8,128)}) %all-gather.11.cloned.1.call-update) | async-done | bytes 8388624 | tf_op jit(solution)/shard_map/all_gather | solution.py:14
  176.6 33.0 %while.17 = (s32[]{:T(128)}, f32[1,8,64,128]{3,2,1,0:T(8,128)S(1)}, s32[]{:T(128)}, f32[32,1,8]{2,1,0:T(1,128)S(1)}, f32[32,1,8,64,128]{4,3,2,1,0:T(8,128)}, /*index=5*/s32[]{:T(128)}, s32[]{:T(128)}, s32[]{:T(128)}, s32[]{:T(128)}) while((s32[]{:T(128)}, f32[1,8,64,128]{3,2,1,0:T(8,128)S(1)}, s32[]{:T(128)}, f32[32,1,8]{2,1,0:T(1,128)S(1)}, ...), condition=%wide.region_5.6_spmd, body=%wide.region_4.5_spmd.sunk | while | flops 131078 | bytes 786683 | solution.py:23
  176.7 1.1 bitcast_add_fusion.5
  177.8 1.1 bitcast_add_fusion.5
  178.9 1.1 bitcast_add_fusion.5
  180.0 1.1 bitcast_add_fusion.5
  181.1 1.1 bitcast_add_fusion.5
  182.2 1.1 bitcast_add_fusion.5
  183.3 1.1 bitcast_add_fusion.5
  184.4 1.1 bitcast_add_fusion.5
  185.5 1.1 bitcast_add_fusion.5
  186.6 1.1 bitcast_add_fusion.5
  187.7 1.1 bitcast_add_fusion.5
  188.8 1.1 bitcast_add_fusion.5
  189.9 1.1 bitcast_add_fusion.5
  191.0 1.1 bitcast_add_fusion.5
  192.1 1.1 bitcast_add_fusion.5
  193.2 1.1 bitcast_add_fusion.5
  194.3 1.1 bitcast_add_fusion.5
  195.4 1.1 bitcast_add_fusion.5
  196.5 1.1 bitcast_add_fusion.5
  197.6 1.1 bitcast_add_fusion.5
  198.7 1.1 bitcast_add_fusion.5
  199.8 1.1 bitcast_add_fusion.5
  200.9 1.1 bitcast_add_fusion.5
  202.0 1.1 bitcast_add_fusion.5
  203.1 1.1 bitcast_add_fusion.5
  204.2 1.1 bitcast_add_fusion.5
  205.3 1.1 bitcast_add_fusion.5
  206.4 1.1 bitcast_add_fusion.5
  207.5 1.1 bitcast_add_fusion.5
  208.6 1.1 bitcast_add_fusion.5
  209.7 0.6 convolution_bitcast_fusion.5
  210.3 0.3 fusion.10
  210.6 0.6 convolution_bitcast_fusion.3
  211.2 0.2 fusion.14
  211.4 0.2 fusion.13
  211.7 2.2 convolution_bitcast_fusion
  213.9 3.5 copy.82
  217.5 100.7 %reduce-scatter.4.cloned.1.call-done = f32[32,768]{1,0:T(8,128)} async-done(((f32[1024,768]{1,0:T(8,128)}), f32[32,768]{1,0:T(8,128)}) %reduce-scatter.4.cloned.1.call-update) | async-done | bytes 98320 | tf_op jit(solution)/shard_map/reduce_scatter | solution.py:164
  318.3 0.3 fusion.6
  318.6 0.7 fusion.8
  319.3 0.3 fusion.9
  319.6 0.8 copy.81
  320.4 59.9 %all-gather.13.cloned.1.call-done = f32[512,768]{1,0:T(8,128)} async-done(((f32[32,768]{1,0:T(8,128)}), f32[512,768]{1,0:T(8,128)}) %all-gather.13.cloned.1.call-update) | async-done | bytes 1572880 | tf_op jit(solution)/shard_map/all_gather | solution.py:172
  380.3 1.5 reduce_sum.25
  381.8 0.6 slice.33
  382.4 0.6 slice.34
  (68 shorter events, 2.1 us)
Async XLA Ops:
  7.2 3.3 copy-start
  7.2 91.2 %all-gather.9.cloned.1.call-start = ((), (), s32[]{:S(2)}) async-start(), calls=%async_computation.1 | async-start | bytes 8650752 | tf_op jit(solution)/shard_map/all_gather | solution.py:14
  12.9 163.7 %all-gather.11.cloned.1.call-start = ((), (), s32[]{:S(2)}) async-start(), calls=%async_computation.2 | async-start | bytes 8650752 | tf_op jit(solution)/shard_map/all_gather | solution.py:14
  14.1 197.6 %copy-start.1 = (bf16[1,128,1024]{2,1,0:T(8,128)(2,1)S(1)}, bf16[1,128,1024]{2,1,0:T(8,128)(2,1)}, u32[]{:S(2)}) copy-start(bf16[1,128,1024]{2,1,0:T(8,128)(2,1)} %param.9) | copy-start | bytes 786436
  15.1 303.1 %reduce-scatter.4.cloned.1.call-start = ((), (), s32[]{:S(2)}) async-start(), calls=%async_computation.4 | async-start | bytes 3244032 | tf_op jit(solution)/shard_map/reduce_scatter | solution.py:164
  217.5 162.8 %all-gather.13.cloned.1.call-start = ((), (), s32[]{:S(2)}) async-start(), calls=%async_computation.3 | async-start | bytes 1671168 | tf_op jit(solution)/shard_map/all_gather | solution.py:172
Sparse Core Ops, SparseCore 0:
  13.0 85.3 all-gather.8
  100.5 76.0 all-gather.10
  217.6 100.6 reduce-scatter.3
  321.6 58.6 all-gather.12
